TPU v7x, 256 devices: a whole 4x4x8 slice. The times are simulated.
256 devices in a mesh: row: 16 (over z_lo, x, core), col: 16 (over z_hi, y).
Axes of the slice: x: 4, y: 4, z: 8 (z_hi: 4, z_lo: 2; z = z_hi * 2 + z_lo), core: 2. Of those that a mesh axis runs over, the one named last changes fastest.
Arguments:
- blocks_inverse: bfloat16 [12288, 12288], P('row', 'col'), as said below
- factor_rows: bfloat16 [2, 6144, 256], P(None, 'row'), may hold values from -0.15234375 to 0.15234375
- block_lists: int32 [2, 48], replicated, may hold values from 0 to 95, as said below
- diag_inverse: float32 [2, 256, 256], replicated, as said below
Outputs:
- column_inverse: float32 [2, 12288, 256], P(None, 'row')
- mirror_inverse: float32 [2, 256, 12288], P(None, None, 'col')
- diagonal_inverse: float32 [2, 256, 256], replicated
Inputs may be any that keep to these rules, and one draw needn't show every extreme that they name: blocks_inverse is exactly symmetric and positive definite. block_lists[s, m] is 2 * m or 2 * m + 1. diag_inverse[s] is symmetric.
All inputs are finite; a program needn't handle non-finite values.
Results may differ from a plain program's by a relative error of at most 0.0003.
Values may be sent and summed in bfloat16 or wider, within the bound.
A program may use at most 64 MiB of HBM per device.

v0:
```python
import jax
import jax.numpy as jnp
from jax import lax
from jax.sharding import PartitionSpec as P

BS = 128


def broadcast(x, axis, root):
    mine = lax.axis_index(axis) == root
    return lax.psum(jnp.where(mine, x, jnp.zeros_like(x)), axis)


def pair_bits(block_lists, first_block, block_count):
    local_lists = lax.dynamic_slice_in_dim(block_lists, first_block // 2, block_count // 2, 1)
    pair_first = 2 * (first_block // 2 + jnp.arange(block_count // 2, dtype=jnp.int32))
    return local_lists - pair_first[None, :]


def expand_pairs(packed, bits):
    sup_count = packed.shape[0]
    feature_count = packed.shape[2]
    pairs = bits.shape[1]
    grouped = packed.reshape(sup_count, pairs, 1, BS, feature_count)
    which = (
        bits[:, :, None, None, None] == jnp.arange(2, dtype=jnp.int32)[None, None, :, None, None]
    )
    dense = jnp.where(which, grouped, jnp.zeros((), packed.dtype))
    return dense.reshape(sup_count, pairs * 2 * BS, feature_count)


def compact_pairs(dense, bits):
    sup_count = dense.shape[0]
    feature_count = dense.shape[2]
    pairs = bits.shape[1]
    grouped = dense.reshape(sup_count, pairs, 2, BS, feature_count)
    chosen = jnp.where(bits[:, :, None, None] == 0, grouped[:, :, 0], grouped[:, :, 1])
    return chosen.reshape(sup_count, pairs * BS, feature_count)


def multiply_each(matrix, stacked):
    results = []
    for sup_index in range(stacked.shape[0]):
        results.append(
            jnp.dot(matrix, stacked[sup_index].astype(jnp.float32), precision=lax.Precision.HIGHEST)
        )
    return jnp.stack(results)


def local(blocks_inverse, factor_rows, block_lists, diag_inverse):
    row_index = lax.axis_index("row")
    col_index = lax.axis_index("col")
    row_blocks = blocks_inverse.shape[0] // BS
    col_blocks = blocks_inverse.shape[1] // BS
    row_bits = pair_bits(block_lists, row_index * row_blocks, row_blocks)
    col_bits = pair_bits(block_lists, col_index * col_blocks, col_blocks)
    packed_length = col_blocks // 2 * BS
    root_row = col_index * col_blocks // row_blocks
    gathered = lax.all_gather(factor_rows, "row", axis=1, tiled=True)
    column_packed = lax.dynamic_slice_in_dim(gathered, col_index * packed_length, packed_length, 1)
    column_dense = expand_pairs(column_packed, col_bits)
    blocks_wide = blocks_inverse.astype(jnp.float32)
    products = multiply_each(blocks_wide, column_dense)
    listed_products = compact_pairs(products, row_bits)
    diagonal_terms = jnp.einsum(
        "srw,srv->swv",
        factor_rows.astype(jnp.float32),
        listed_products,
        precision=lax.Precision.HIGHEST,
    )
    diagonal_inverse = diag_inverse + lax.psum(diagonal_terms, ("row", "col"))
    row_total = lax.psum(listed_products, "col")
    column_inverse = -expand_pairs(row_total, row_bits)
    mirror_total = broadcast(row_total, "row", root_row)
    mirror_inverse = jnp.transpose(-expand_pairs(mirror_total, col_bits), (0, 2, 1))
    return (column_inverse, mirror_inverse, diagonal_inverse)


def solution(mesh):
    return jax.shard_map(
        local,
        mesh=mesh,
        in_specs=(P("row", "col"), P(None, "row", None), P(), P()),
        out_specs=(P(None, "row", None), P(None, None, "col"), P()),
        check_vma=False,
    )
```

profile of v0, /device:TPU:1, one launch (start us, length us, event | category | flops | bytes accessed | tf_op | source)
XLA Modules:
  0.0 641.8 jit_solution(4474671392308871341)
XLA Ops:
  7.2 0.0 copy-start
  7.2 0.0 all-gather.2.cloned.1.call-start
  7.2 0.7 all-gather.2.cloned.1.call-update
  8.0 0.8 broadcast_compare_fusion
  8.7 0.1 broadcast_bitcast_fusion
  8.8 0.8 dynamic-slice_subtract_fusion
  9.6 0.1 iota_compare_fusion
  9.6 49.3 %all-gather.2.cloned.1.call-done = bf16[2,6144,256]{2,1,0:T(8,128)(2,1)} async-done(((bf16[2,384,256]{2,1,0:T(8,128)(2,1)}), bf16[2,6144,256]{2,1,0:T(8,128)(2,1)}) %all-gather.2.cloned.1.call-update) | async-done | bytes 6291472 | tf_op jit(solution)/shard_map/all_gather | solution.py:59
  59.0 1.0 constant_dynamic-slice_fusion
  60.0 0.1 broadcast_select_fusion
  60.1 0.8 fusion.1
  60.9 0.0 copy-done
  60.9 0.5 convolution_bitcast_fusion.1
  61.4 0.4 stack.9
  61.9 1.5 convolution_bitcast_fusion
  63.4 0.4 stack.10
  63.8 0.3 constant_dynamic-update-slice_fusion.1
  64.1 0.3 constant_dynamic-update-slice_fusion
  64.4 1.2 fusion
  65.6 1.0 copy.11
  66.6 1.0 copy.10
  67.6 0.2 broadcast_select_fusion.2
  67.8 0.0 copy-start.1
  67.8 3.0 convolution_bitcast_fusion.2
  70.8 0.0 all-reduce.4.cloned.1.call-start
  70.8 0.0 copy-done.1
  70.8 0.7 all-reduce.4.cloned.1.call-update
  71.5 0.0 copy-start.3
  71.5 0.0 all-reduce.8.cloned.1.call-start
  71.6 0.7 all-reduce.8.cloned.1.call-update
  72.2 0.0 all-reduce.6.cloned.1.call-start
  72.3 160.2 %all-reduce.4.cloned.1.call-done = f32[2,384,256]{2,1,0:T(8,128)} async-done(((f32[2,384,256]{2,1,0:T(8,128)}), f32[2,384,256]{2,1,0:T(8,128)}) %all-reduce.4.cloned.1.call-update) | async-done | bytes 786448 | tf_op jit(solution)/shard_map/psum | solution.py:72
  232.5 0.9 broadcast_select_fusion.1
  233.5 0.0 all-reduce.6.cloned.1.call-update
  233.5 0.1 iota_compare_fusion.1
  233.6 0.1 broadcast_in_dim.93
  233.7 0.1 broadcast_in_dim.107
  233.8 0.0 copy-done.3
  233.8 0.2 copy.15
  234.0 0.0 copy-start.2
  234.0 267.5 %all-reduce.8.cloned.1.call-done = f32[2,256,256]{1,2,0:T(8,128)} async-done(((f32[2,256,256]{1,2,0:T(8,128)}), f32[2,256,256]{1,2,0:T(8,128)}) %all-reduce.8.cloned.1.call-update) | async-done | bytes 524304 | tf_op jit(solution)/shard_map/psum | solution.py:71
  501.5 1.1 add.48
  502.6 1.0 copy.17
  503.6 0.0 copy-done.2
  503.6 0.4 copy.12
  504.0 1.7 broadcast_in_dim.104
  505.7 2.5 broadcast_in_dim.105
  508.2 1.3 select_negate_fusion
  509.5 3.0 copy.16
  512.5 115.7 %all-reduce.6.cloned.1.call-done = f32[2,3,128,256]{3,2,1,0:T(8,128)} async-done(((f32[2,3,128,256]{3,2,1,0:T(8,128)}), f32[2,3,128,256]{3,2,1,0:T(8,128)}) %all-reduce.6.cloned.1.call-update) | async-done | bytes 786448 | tf_op jit(solution)/shard_map/psum | solution.py:11
  628.2 1.5 copy.13
  629.8 1.7 broadcast_in_dim.112
  631.4 2.5 broadcast_in_dim.113
  634.0 1.3 negate_bitcast_fusion
  (5 shorter events, 0.1 us)
Async XLA Ops:
  7.2 53.8 %copy-start = (bf16[768,768]{1,0:T(8,128)(2,1)S(1)}, bf16[768,768]{1,0:T(8,128)(2,1)}, u32[]{:S(2)}) copy-start(bf16[768,768]{1,0:T(8,128)(2,1)} %param.4) | copy-start | bytes 3538948
  7.2 51.8 %all-gather.2.cloned.1.call-start = ((), (), s32[]{:S(2)}) async-start(), calls=%async_computation | async-start | bytes 6684672 | tf_op jit(solution)/shard_map/all_gather | solution.py:59
  67.8 3.0 copy-start.1
  70.8 161.8 %all-reduce.4.cloned.1.call-start = ((), (), s32[]{:S(2)}) async-start(), calls=%async_computation.1 | async-start | bytes 1572864 | tf_op jit(solution)/shard_map/psum | solution.py:72
  71.5 162.3 %copy-start.3 = (f32[2,256,256]{2,1,0:T(8,128)S(1)}, f32[2,256,256]{2,1,0:T(8,128)}, u32[]{:S(2)}) copy-start(f32[2,256,256]{2,1,0:T(8,128)} %param.7) | copy-start | bytes 1572868
  71.5 430.0 %all-reduce.8.cloned.1.call-start = ((), (), s32[]{:S(2)}) async-start(), calls=%async_computation.3 | async-start | bytes 1048576 | tf_op jit(solution)/shard_map/psum | solution.py:71
  72.2 556.0 %all-reduce.6.cloned.1.call-start = ((), (), s32[]{:S(2)}) async-start(), calls=%async_computation.2 | async-start | bytes 1572864 | tf_op jit(solution)/shard_map/psum | solution.py:11
  234.0 269.6 %copy-start.2 = (f32[2,384,256]{2,1,0:T(8,128)S(1)}, f32[2,384,256]{2,1,0:T(8,128)}, u32[]{:S(2)}) copy-start(f32[2,384,256]{2,1,0:T(8,128)} %all-reduce.4.cloned.1.call-done) | copy-start | bytes 2359300
Sparse Core Ops, SparseCore 0:
  9.8 49.1 all-gather.1
  74.8 157.7 all-reduce.3
  238.6 262.8 all-reduce.7
  504.0 124.2 all-reduce.5
where the time goes:
time: 642 us
  waiting for transfers between devices  595 us (93%)
  local copies, waits for them, and re-layouts  21.3 us (3%)
  between operations  14 us (2%)
  other arithmetic  6.57 us (1%)
    psum x1, waiting for transfers between devices, local(): diagonal_inverse = diag_inverse + lax.psum(diagonal_terms, ('row', 'col'))  268 us
    psum x1, waiting for transfers between devices, local(): row_total = lax.psum(listed_products, 'col')  160 us
    psum x1, waiting for transfers between devices, broadcast(): return lax.psum(jnp.where(mine, x, jnp.zeros_like(x)), axis)  116 us
    all_gather x1, waiting for transfers between devices, local(): gathered = lax.all_gather(factor_rows, 'row', axis=1, tiled=True)  49.3 us
  transfers between devices with their start and end apart: 4, of which 4 were waited for; matrix products, arithmetic and copies ran while one was open for 2% of the time, Pallas kernels for 0%

commit v1 on v0

--- a/solution.py
+++ b/solution.py
@@ -68,7 +68,7 @@
         listed_products,
         precision=lax.Precision.HIGHEST,
     )
-    diagonal_inverse = diag_inverse + lax.psum(diagonal_terms, ("row", "col"))
+    diagonal_inverse = diag_inverse + lax.psum(lax.psum(diagonal_terms, "row"), "col")
     row_total = lax.psum(listed_products, "col")
     column_inverse = -expand_pairs(row_total, row_bits)
     mirror_total = broadcast(row_total, "row", root_row)

time: 642 us -> 509 us (0.79)
  waiting for transfers between devices: 595 us -> 464 us
    psum x1, waiting for transfers between devices: 268 us -> 124 us  [local(): lax.psum(diagonal_terms, 'row')]
    psum x1, waiting for transfers between devices: 116 us -> 124 us  [broadcast(): return lax.psum(jnp.where(mine, x, jnp.zeros_like(x)), axis)]
where the time goes in v1:
time: 509 us
  waiting for transfers between devices  464 us (91%)
  local copies, waits for them, and re-layouts  22.1 us (4%)
  between operations  14 us (3%)
  other arithmetic  5.54 us (1%)
    psum x1, waiting for transfers between devices, local(): row_total = lax.psum(listed_products, 'col')  166 us
    psum x1, waiting for transfers between devices, broadcast(): return lax.psum(jnp.where(mine, x, jnp.zeros_like(x)), axis)  124 us
    psum x1, waiting for transfers between devices, local(): lax.psum(diagonal_terms, 'row')  124 us
    all_gather x1, waiting for transfers between devices, local(): gathered = lax.all_gather(factor_rows, 'row', axis=1, tiled=True)  49.3 us
  transfers between devices with their start and end apart: 4, of which 4 were waited for; matrix products, arithmetic and copies ran while one was open for 2% of the time, Pallas kernels for 0%

profile of v1, /device:TPU:1, one launch (start us, length us, event | category | flops | bytes accessed | tf_op | source)
XLA Modules:
  0.0 509.0 jit_solution(12133648193900890622)
XLA Ops:
  7.2 0.0 copy-start
  7.2 0.0 all-gather.2.cloned.1.call-start
  7.2 0.7 all-gather.2.cloned.1.call-update
  7.9 0.0 all-reduce.7.cloned.1.call-start
  8.0 0.8 broadcast_compare_fusion
  8.8 0.1 broadcast_bitcast_fusion
  8.9 0.8 dynamic-slice_subtract_fusion
  9.6 0.1 iota_compare_fusion
  9.7 49.3 %all-gather.2.cloned.1.call-done = bf16[2,6144,256]{2,1,0:T(8,128)(2,1)} async-done(((bf16[2,384,256]{2,1,0:T(8,128)(2,1)}), bf16[2,6144,256]{2,1,0:T(8,128)(2,1)}) %all-gather.2.cloned.1.call-update) | async-done | bytes 6291472 | tf_op jit(solution)/shard_map/all_gather | solution.py:59
  59.0 1.0 constant_dynamic-slice_fusion
  60.0 0.1 broadcast_select_fusion
  60.1 0.8 fusion.1
  60.9 0.0 copy-done
  60.9 0.5 convolution_bitcast_fusion.1
  61.4 0.4 stack.9
  61.9 1.5 convolution_bitcast_fusion
  63.4 0.4 stack.10
  63.8 0.3 constant_dynamic-update-slice_fusion.1
  64.1 0.3 constant_dynamic-update-slice_fusion
  64.4 1.2 fusion
  65.6 1.0 copy.11
  66.6 1.0 copy.10
  67.6 0.0 copy-start.3
  67.6 0.2 broadcast_select_fusion.2
  67.8 0.8 copy-done.3
  68.6 0.0 copy-start.1
  68.6 1.7 convolution_bitcast_fusion.2
  70.3 0.0 all-reduce.7.cloned.1.call-update
  70.3 0.0 all-reduce.9.cloned.1.call-start
  70.4 123.6 %all-reduce.7.cloned.1.call-done = f32[2,256,256]{1,2,0:T(8,128)} async-done(((f32[2,256,256]{1,2,0:T(8,128)}), f32[2,256,256]{1,2,0:T(8,128)}) %all-reduce.7.cloned.1.call-update) | async-done | bytes 524304 | tf_op jit(solution)/shard_map/psum | solution.py:71
  194.0 0.0 copy-start.5
  194.0 0.0 copy-done.1
  194.0 0.0 all-reduce.9.cloned.1.call-update
  194.0 0.0 all-reduce.5.cloned.1.call-start
  194.1 166.2 %all-reduce.9.cloned.1.call-done = (f32[2,384,256]{2,1,0:T(8,128)}, f32[2,256,256]{1,2,0:T(8,128)}) async-done(((f32[2,384,256]{2,1,0:T(8,128)}, f32[2,256,256]{1,2,0:T(8,128)}), (f32[2,384,256]{2,1,0:T(8,128)}, f32[2,256,256]{1,2,0:T(8,128)})) %all-reduce.9.cloned.1.call-update) | async-done | bytes 1310736 | tf_op jit(solution)/shard_map/psum | solution.py:72
  360.3 0.0 copy-start.4
  360.3 0.9 broadcast_select_fusion.1
  361.2 0.0 all-reduce.5.cloned.1.call-update
  361.3 0.1 iota_compare_fusion.1
  361.3 0.1 broadcast_in_dim.93
  361.4 0.1 broadcast_in_dim.107
  361.5 0.0 copy-done.5
  361.5 0.2 copy.15
  361.8 0.0 copy-start.2
  361.8 0.0 copy-done.4
  361.8 0.1 add.50
  361.8 1.0 copy.17
  362.8 0.0 copy-done.2
  362.9 0.4 copy.12
  363.3 1.7 broadcast_in_dim.104
  365.0 2.5 broadcast_in_dim.105
  367.5 1.3 select_negate_fusion
  368.8 3.0 copy.16
  371.8 123.7 %all-reduce.5.cloned.1.call-done = f32[2,3,128,256]{3,2,1,0:T(8,128)} async-done(((f32[2,3,128,256]{3,2,1,0:T(8,128)}), f32[2,3,128,256]{3,2,1,0:T(8,128)}) %all-reduce.5.cloned.1.call-update) | async-done | bytes 786448 | tf_op jit(solution)/shard_map/psum | solution.py:11
  495.5 1.5 copy.13
  497.0 1.7 broadcast_in_dim.112
  498.7 2.5 broadcast_in_dim.113
  501.2 1.3 negate_bitcast_fusion
  (5 shorter events, 0.1 us)
Async XLA Ops:
  7.2 53.8 %copy-start = (bf16[768,768]{1,0:T(8,128)(2,1)S(1)}, bf16[768,768]{1,0:T(8,128)(2,1)}, u32[]{:S(2)}) copy-start(bf16[768,768]{1,0:T(8,128)(2,1)} %param.4) | copy-start | bytes 3538948
  7.2 51.8 %all-gather.2.cloned.1.call-start = ((), (), s32[]{:S(2)}) async-start(), calls=%async_computation | async-start | bytes 6684672 | tf_op jit(solution)/shard_map/all_gather | solution.py:59
  7.9 186.1 %all-reduce.7.cloned.1.call-start = ((), (), s32[]{:S(2)}) async-start(), calls=%async_computation.2 | async-start | bytes 1048576 | tf_op jit(solution)/shard_map/psum | solution.py:71
  67.6 1.0 copy-start.3
  68.6 125.3 %copy-start.1 = (f32[2,384,256]{2,1,0:T(8,128)}, f32[2,384,256]{2,1,0:T(8,128)S(1)}, u32[]{:S(2)}) copy-start(f32[2,384,256]{2,1,0:T(8,128)S(1)} %broadcast_select_fusion.2) | copy-start | bytes 2359300
  70.3 290.0 %all-reduce.9.cloned.1.call-start = ((), (), s32[]{:S(2)}) async-start(), calls=%async_computation.3 | async-start | bytes 2621440 | tf_op jit(solution)/shard_map/psum | solution.py:72
  194.0 167.6 %copy-start.5 = (f32[2,256,256]{2,1,0:T(8,128)S(1)}, f32[2,256,256]{2,1,0:T(8,128)}, u32[]{:S(2)}) copy-start(f32[2,256,256]{2,1,0:T(8,128)} %param.7) | copy-start | bytes 1572868
  194.0 301.5 %all-reduce.5.cloned.1.call-start = ((), (), s32[]{:S(2)}) async-start(), calls=%async_computation.1 | async-start | bytes 1572864 | tf_op jit(solution)/shard_map/psum | solution.py:11
  360.3 1.5 copy-start.4
  361.8 1.1 copy-start.2
Sparse Core Ops, SparseCore 0:
  9.8 49.1 all-gather.1
  70.4 123.4 all-reduce.6
  197.3 163.0 all-reduce.8
  362.8 132.6 all-reduce.4
